TPU v7x, 256 devices: a whole 4x4x8 slice. The times are simulated.
256 devices in a mesh: chain: 2 (over core), leaf: 16 (over y, x), head: 8 (over z).
Axes of the slice: x: 4, y: 4, z: 8, core: 2. Of those that a mesh axis runs over, the one named last changes fastest.
Arguments:
- query_in: bfloat16 [16384, 16, 128], P(('chain', 'leaf'), 'head'), may hold values from -6 to 6
- key_in: bfloat16 [16384, 16, 128], P(('chain', 'leaf'), 'head'), may hold values from -120 to 120
- value_in: bfloat16 [16384, 16, 128], P(('chain', 'leaf'), 'head'), may hold values from -6 to 6
- gate_in: bfloat16 [16384, 16, 128], P(('chain', 'leaf'), 'head'), may hold values from -6 to 6
- write_strength: float32 [16, 16384], P('head', ('chain', 'leaf')), as said below
- log_decay: float32 [16, 16384], P('head', ('chain', 'leaf')), as said below
- doc_resets: int32 [256], P(('chain', 'leaf')), may hold values from 0 to 1, as said below
- conv_weight: float32 [3, 4, 16, 128], P(None, None, 'head'), may hold values from -3 to 3
- output_norm_gain: float32 [128], replicated, may hold values from 0.25 to 1.75
- output_projection_weight: bfloat16 [2048, 4096], P(None, 'head'), may hold values from -0.125 to 0.125
Outputs:
- mixed: bfloat16 [16384, 4096], P(('chain', 'leaf'), 'head')
Inputs may be any that keep to these rules, and one draw needn't show every extreme that they name: `write_strength`: strictly positive. `log_decay`: strictly negative. `doc_resets`: at least one block of every draw starts a document.
All inputs are finite; a program needn't handle non-finite values.
Results may differ from a plain program's by a relative error of at most 0.0064.
Values may be sent and summed in bfloat16 or wider, within the bound.
A program may use at most 64 MiB of HBM per device.

v0:
```python
import jax
import jax.numpy as jnp
from jax import lax
from jax.sharding import PartitionSpec as P

BLOCK = 64


highest = lax.Precision.HIGHEST
epsilon = 1e-06


def from_behind(value, axis, steps):
    count = lax.axis_size(axis)
    initial, last = (max(0, -steps), min(count, count - steps))
    return lax.ppermute(value, axis, [(source, source + steps) for source in range(initial, last)])


def prefix(part, axis, combine, identity):
    place = lax.axis_index(axis)
    gathered = jax.tree.map(lambda a: lax.all_gather(a, axis), part)
    state = jax.tree.map(lambda a, e: jnp.zeros_like(a) + jnp.asarray(e, a.dtype), part, identity)

    def one(lap, state):
        return combine(
            state, jax.tree.map(lambda a: lax.dynamic_index_in_dim(a, lap, 0, False), gathered)
        )

    return lax.fori_loop(0, place, one, state)


def from_root(shard, axis, root):
    mine = lax.axis_index(axis) == root
    return lax.psum(jnp.where(mine, shard, jnp.zeros_like(shard)), axis)


def unit_rows(matrix):
    return matrix / jnp.sqrt(jnp.sum(matrix * matrix, axis=-1, keepdims=True) + epsilon)


def chain_pair(earlier, later_pair):
    joined = jnp.einsum("...ij,...jk->...ik", later_pair[0], earlier[0], precision=highest)
    carried = (
        jnp.einsum("...ij,...jk->...ik", later_pair[0], earlier[1], precision=highest)
        + later_pair[1]
    )
    return (joined, carried)


def causal_filter(signal, rim_rows, weights):
    kernel = weights.shape[0]
    length = signal.shape[0]
    padded = jnp.concatenate([rim_rows, signal], axis=0)
    running = weights[0] * padded[0:length]
    for offset in range(1, kernel):
        running = running + weights[offset] * padded[offset : offset + length]
    return jax.nn.silu(running)


def on_device(
    query_in,
    key_in,
    value_in,
    gate_in,
    write_strength,
    log_decay,
    doc_resets,
    conv_weight,
    output_norm_gain,
    output_projection_weight,
):
    length, head_count, depth_k = query_in.shape
    value_width = value_in.shape[2]
    kernel = conv_weight.shape[1]
    tail_rows = jnp.stack(
        [
            query_in[length - kernel + 1 :],
            key_in[length - kernel + 1 :],
            value_in[length - kernel + 1 :],
        ]
    )
    rim_rows = from_behind(tail_rows, ("chain", "leaf"), 1)
    query_conv = causal_filter(query_in, rim_rows[0], conv_weight[0])
    key_conv = causal_filter(key_in, rim_rows[1], conv_weight[1])
    value_conv = causal_filter(value_in, rim_rows[2], conv_weight[2])
    query_unit = (unit_rows(query_conv) * depth_k ** (-0.5)).astype(jnp.bfloat16)
    key_unit = unit_rows(key_conv).astype(jnp.bfloat16)
    value_act = value_conv.astype(jnp.bfloat16)
    blocks = length // BLOCK
    query_blk = query_unit.reshape(blocks, BLOCK, head_count, depth_k)
    key_blk = key_unit.reshape(blocks, BLOCK, head_count, depth_k)
    value_blk = value_act.reshape(blocks, BLOCK, head_count, value_width)
    key_gram = jnp.einsum("nthe,nshe->nhts", key_blk, key_blk, preferred_element_type=jnp.float32)
    query_gram = jnp.einsum(
        "nthe,nshe->nhts", query_blk, key_blk, preferred_element_type=jnp.float32
    )
    strength = write_strength.reshape(head_count, blocks, BLOCK).transpose(1, 0, 2)
    decays = log_decay.reshape(head_count, blocks, BLOCK).transpose(1, 0, 2)
    row_index = lax.broadcasted_iota(jnp.int32, (BLOCK, BLOCK), 0)
    col_index = lax.broadcasted_iota(jnp.int32, (BLOCK, BLOCK), 1)
    strict_mask = row_index > col_index
    causal_mask = row_index >= col_index
    cumulative = jnp.cumsum(decays, axis=-1)
    spread_log = cumulative[..., :, None] - cumulative[..., None, :]
    fading = jnp.where(causal_mask, jnp.exp(jnp.where(causal_mask, spread_log, 0.0)), 0.0)
    growth = jnp.exp(cumulative)
    lower = jnp.where(strict_mask, strength[..., :, None] * fading * key_gram, 0.0)
    mixing = fading * query_gram
    query_float = jnp.transpose(query_blk, (0, 2, 1, 3)).astype(jnp.float32)
    key_float = jnp.transpose(key_blk, (0, 2, 1, 3)).astype(jnp.float32)
    value_float = jnp.transpose(value_blk, (0, 2, 1, 3)).astype(jnp.float32)
    targets = jnp.concatenate(
        [strength[..., None] * value_float, (strength * growth)[..., None] * key_float], axis=-1
    )
    solved = jax.scipy.linalg.solve_triangular(
        jnp.eye(BLOCK, dtype=jnp.float32) + lower, targets, lower=True, unit_diagonal=True
    )
    local_values = solved[..., :value_width]
    write_keys = solved[..., value_width:]
    tail_fade = jnp.exp(cumulative[..., -1:] - cumulative)
    decayed_addresses = tail_fade[..., None] * key_float
    key_eye = jnp.eye(depth_k, dtype=jnp.float32)
    keep_mat = (1 - doc_resets).astype(jnp.float32)[:, None, None, None]
    transition = keep_mat * (
        growth[..., -1, None, None] * key_eye
        - jnp.einsum("nhce,nhcf->nhef", decayed_addresses, write_keys, precision=highest)
    )
    addition = jnp.einsum("nhce,nhcf->nhef", decayed_addresses, local_values, precision=highest)
    query_eff = keep_mat * (
        growth[..., None] * query_float
        - jnp.einsum("nhts,nhse->nhte", mixing, write_keys, precision=highest)
    )
    own_output = jnp.einsum("nhts,nhsf->nhtf", mixing, local_values, precision=highest)
    prefix_trans, prefix_state = lax.associative_scan(chain_pair, (transition, addition), axis=0)
    start_trans = jnp.concatenate(
        [jnp.broadcast_to(key_eye, (1, head_count, depth_k, depth_k)), prefix_trans[:-1]], axis=0
    )
    start_state = jnp.concatenate(
        [jnp.zeros((1, head_count, depth_k, value_width), jnp.float32), prefix_state[:-1]], axis=0
    )
    device_trans = prefix_trans[-1]
    device_state = prefix_state[-1]
    partial_out = own_output + jnp.einsum(
        "nhtd,nhdf->nhtf", query_eff, start_state, precision=highest
    )
    reach_map = jnp.einsum("nhtd,nhde->nhte", query_eff, start_trans, precision=highest)
    identity_pair = (
        jnp.broadcast_to(key_eye, (head_count, depth_k, depth_k)),
        jnp.zeros((head_count, depth_k, value_width), jnp.float32),
    )
    leaf_trans, leaf_state = prefix((device_trans, device_state), "leaf", chain_pair, identity_pair)
    through = chain_pair((leaf_trans, leaf_state), (device_trans, device_state))
    group_pair = from_root(jnp.stack(through), "leaf", lax.axis_size("leaf") - 1)
    outer_trans, outer_state = prefix(
        (group_pair[0], group_pair[1]), "chain", chain_pair, identity_pair
    )
    incoming = jnp.einsum("hij,hjk->hik", leaf_trans, outer_state, precision=highest) + leaf_state
    core = partial_out + jnp.einsum("nhte,hef->nhtf", reach_map, incoming, precision=highest)
    core = jnp.transpose(core, (0, 2, 1, 3)).reshape(length, head_count, value_width)
    scale_rms = jnp.sqrt(jnp.mean(core * core, axis=-1, keepdims=True) + epsilon)
    normed = (
        core / scale_rms * output_norm_gain * jax.nn.silu(gate_in.astype(jnp.float32))
    ).astype(jnp.bfloat16)
    shard_piece = lax.all_gather(normed, "head", axis=1, tiled=True)
    count = shard_piece.shape[1]
    flat_piece = shard_piece.reshape(shard_piece.shape[0], count * value_width)
    mixed = jnp.dot(flat_piece, output_projection_weight, preferred_element_type=jnp.float32)
    return mixed.astype(jnp.bfloat16)


def solution(mesh):
    return jax.shard_map(
        on_device,
        mesh=mesh,
        in_specs=(
            P(("chain", "leaf"), "head", None),
            P(("chain", "leaf"), "head", None),
            P(("chain", "leaf"), "head", None),
            P(("chain", "leaf"), "head", None),
            P("head", ("chain", "leaf")),
            P("head", ("chain", "leaf")),
            P(("chain", "leaf")),
            P(None, None, "head", None),
            P(),
            P(None, "head"),
        ),
        out_specs=P(("chain", "leaf"), "head"),
        check_vma=False,
    )
```

profile of v0, /device:TPU:24, one launch (start us, length us, event | category | flops | bytes accessed | tf_op | source)
XLA Modules:
  0.0 429.3 jit_solution(7964937536318797410)
XLA Ops:
  6.5 1.1 copy.145
  10.4 3.4 collective-permute-start
  13.9 1.3 subtract_convert_fusion
  17.3 1.4 slice_bitcast_fusion.23
  20.1 1.2 fusion.18
  21.3 79.4 %custom-call.4 = f32[8,2,1,64,64]{3,4,2,1,0:T(8,128)S(1)} custom-call(f32[8,2,1,64,64]{4,3,2,1,0:T(8,128)} %fusion.18), custom_call_target="InvertDiagBlocksLowerTriangular" | custom-call | tf_op jit(solution)/shard_map/jit(_solve_triangular)/vmap(vmap())/triangular_solve | solution.py:115
  102.2 2.0 fusion.37
  104.2 2.0 fusion.10
  110.4 3.7 pad.41
  114.2 3.8 pad.42
  117.9 2.0 add.203
  120.0 5.7 %pad.185 = f32[7,2,128,128]{3,2,1,0:T(8,128)} pad(f32[4,2,128,128]{3,2,1,0:T(8,128)} %add.203, f32[]{:T(128)} %constant.56.clone.1), padding=0_0_1x0_0_0x0_0_0x0_0_0 | pad | bytes 1441796
  125.6 1.6 slice.474
  129.1 1.2 convolution_bitcast_fusion.2
  130.3 2.1 pad.47
  133.3 2.2 pad.48
  135.5 2.1 add.209
  137.6 5.7 %pad.50 = f32[8,2,128,128]{3,2,1,0:T(8,128)} pad(f32[4,2,128,128]{3,2,1,0:T(8,128)} %add.209, f32[]{:T(128)} %constant.56.clone.1), padding=1_0_1x0_0_0x0_0_0x0_0_0 | pad | bytes 1572868 | tf_op jit(solution)/shard_map/pad | solution.py:134
  143.3 1.6 fusion.50
  145.8 5.7 %pad.49 = f32[8,2,128,128]{3,2,1,0:T(8,128)} pad(f32[4,2,128,128]{3,2,1,0:T(8,128)} %pad_maximum_fusion.1, f32[]{:T(128)} %constant.56.clone.1), padding=0_1_1x0_0_0x0_0_0x0_0_0 | pad | bytes 1572868 | tf_op jit(solution)/shard_map/pad | solution.py:134
  151.6 1.6 slice_add_fusion.1
  153.3 5.8 %pad.44 = f32[8,2,128,128]{3,2,1,0:T(8,128)} pad(f32[4,2,128,128]{3,2,1,0:T(8,128)} %add.203, f32[]{:T(128)} %constant.56.clone.1), padding=1_0_1x0_0_0x0_0_0x0_0_0 | pad | bytes 1572868 | tf_op jit(solution)/shard_map/pad | solution.py:134
  159.1 5.7 %pad.84 = f32[7,2,128,128]{3,2,1,0:T(8,128)} pad(f32[4,2,128,128]{3,2,1,0:T(8,128)} %pad_maximum_fusion.1, f32[]{:T(128)} %constant.56.clone.1), padding=0_0_1x0_0_0x0_0_0x0_0_0 | pad | bytes 1441796 | tf_op jit(solution)/shard_map/slice | solution.py:136
  164.8 1.8 convolution_add_fusion.4
  167.5 5.8 %pad.43 = f32[8,2,128,128]{3,2,1,0:T(8,128)} pad(f32[4,2,128,128]{3,2,1,0:T(8,128)} %pad_maximum_fusion, f32[]{:T(128)} %constant.56.clone.1), padding=0_1_1x0_0_0x0_0_0x0_0_0 | pad | bytes 1572868 | tf_op jit(solution)/shard_map/pad | solution.py:134
  173.2 2.0 multiply_reduce_fusion.2
  177.5 1.9 fusion.27
  179.4 1.1 slice_add_fusion
  180.5 50.7 %all-gather.4.cloned.1.call-done = f32[16,2,128,128]{3,2,1,0:T(8,128)} async-done(((f32[1,2,128,128]{3,2,1,0:T(8,128)}), f32[16,2,128,128]{3,2,1,0:T(8,128)}) %all-gather.4.cloned.1.call-update) | async-done | bytes 2097168 | tf_op jit(solution)/shard_map/all_gather | solution.py:21
  231.2 29.9 %while.24 = (s32[]{:T(128)}, f32[2,128,128]{2,1,0:T(8,128)S(1)}, f32[2,128,128]{2,1,0:T(8,128)S(1)}, s32[]{:T(128)}, f32[16,2,128,128]{3,2,1,0:T(8,128)}, /*inde...) while((s32[]{:T(128)}, f32[2,128,128]{2,1,0:T(8,128)S(1)}, f32[2,128,128]{2,1,0:T(8,128)S(1)}, ...), condition=%wide.region_4.5_spmd, body=%wide.region_3.4_spmd.sunk | while | flops 100696064 | bytes 1442955 | solution.py:29
  231.3 1.2 convolution_add_fusion.10
  232.5 1.2 fusion.127
  233.8 1.2 convolution_add_fusion.10
  235.0 1.2 fusion.127
  236.2 1.2 convolution_add_fusion.10
  237.5 1.2 fusion.127
  238.7 1.2 convolution_add_fusion.10
  240.0 1.2 fusion.127
  241.2 1.2 convolution_add_fusion.10
  242.5 1.2 fusion.127
  243.7 1.2 convolution_add_fusion.10
  245.0 1.2 fusion.127
  246.2 1.2 convolution_add_fusion.10
  247.4 1.2 fusion.127
  248.7 1.2 convolution_add_fusion.10
  249.9 1.2 fusion.127
  251.2 1.2 convolution_add_fusion.10
  252.4 1.2 fusion.127
  253.7 1.2 convolution_add_fusion.10
  254.9 1.2 fusion.127
  256.1 1.2 convolution_add_fusion.10
  257.4 1.2 fusion.127
  258.6 1.2 convolution_add_fusion.10
  259.9 1.2 fusion.127
  261.1 1.2 fusion.20
  263.4 2.5 fusion.46
  265.8 97.9 %all-reduce.15.cloned.1.call-done = f32[2,2,128,128]{3,2,1,0:T(8,128)} async-done(((f32[2,2,128,128]{3,2,1,0:T(8,128)}), f32[2,2,128,128]{3,2,1,0:T(8,128)}) %all-reduce.15.cloned.1.call-update) | async-done | bytes 262160 | tf_op jit(solution)/shard_map/psum | solution.py:34
  364.7 2.0 all_gather.18
  366.7 2.0 all_gather.17
  369.0 1.7 convolution_bitcast_fusion
  370.8 2.2 multiply_reduce_fusion
  374.1 41.1 %all-gather.8.cloned.1.call-done = bf16[512,16,128]{2,0,1:T(8,128)(2,1)} async-done(((bf16[512,2,128]{2,0,1:T(8,128)(2,1)}), bf16[512,16,128]{2,0,1:T(8,128)(2,1)}) %all-gather.8.cloned.1.call-update) | async-done | bytes 2097168 | tf_op jit(solution)/shard_map/all_gather | solution.py:164
  415.2 3.9 copy.174
  419.1 3.7 convolution_convert_fusion
  (171 shorter events, 22.3 us)
Async XLA Ops:
  6.5 412.6 %copy-start = (bf16[2048,512]{1,0:T(8,128)(2,1)S(1)}, bf16[2048,512]{1,0:T(8,128)(2,1)}, u32[]{:S(2)}) copy-start(bf16[2048,512]{1,0:T(8,128)(2,1)} %param.23) | copy-start | bytes 6291460
  6.5 173.9 %all-gather.6.cloned.1.call-start = ((), (), s32[]{:S(2)}) async-start(), calls=%async_computation.1 | async-start | bytes 2228224 | tf_op jit(solution)/shard_map/all_gather | solution.py:21
  7.7 0.7 copy-start.18
  10.4 8.7 %collective-permute-start = (bf16[3,3,2,128]{3,1,2,0:T(4,128)(2,1)S(1)}, bf16[3,3,2,128]{3,1,2,0:T(4,128)(2,1)S(1)}, u32[]{:S(2)}, u32[]{:S(2)}) collective-permute-start(bf16[3,3,2,128]{3,1,2,0:T(4,128)(2,1)S(1)} %pad_maximum_fusion.7), channel_id=1, source_target_pairs={{0,8},{8,16},{16,24},{24,32},{32,40},{40,48},{48,56},{56,64},{64,7... | collective-permute-start | bytes 13832 | tf_op jit(solution)/shard_map/ppermute | solution.py:16
  13.8 7.4 %copy-start.23 = (pred[64,64]{1,0:T(8,128)(4,1)}, pred[64,64]{1,0:T(8,128)(4,1)S(1)}, u32[]{:S(2)}) copy-start(pred[64,64]{1,0:T(8,128)(4,1)S(1)} %get-tuple-element.137) | copy-start | bytes 12292
  13.9 90.3 %copy-start.19 = (f32[128,128]{1,0:T(8,128)}, f32[128,128]{1,0:T(8,128)S(1)}, u32[]{:S(2)}) copy-start(f32[128,128]{1,0:T(8,128)S(1)} %fusion.87) | copy-start | bytes 196612
  18.9 2.4 copy-start.25
  20.1 84.1 %copy-start.6 = (bf16[512,2,128]{2,0,1:T(8,128)(2,1)}, bf16[512,2,128]{2,0,1:T(8,128)(2,1)S(1)}, u32[]{:S(2)}) copy-start(bf16[512,2,128]{2,0,1:T(8,128)(2,1)S(1)} %divide_convert_fusion) | copy-start | bytes 786436
  101.1 3.1 copy-start.31
  102.1 4.7 %copy-start.1 = (f32[8,2,64,256]{3,2,1,0:T(8,128)}, f32[8,2,64,256]{3,2,1,0:T(8,128)S(1)}, u32[]{:S(2)}) copy-start(f32[8,2,64,256]{3,2,1,0:T(8,128)S(1)} %fusion.23) | copy-start | bytes 3145732
  104.1 3.2 copy-start.8
  106.9 2.1 copy-start.3
  120.0 10.3 %slice-start = ((f32[4,2,128,128]{3,2,1,0:T(8,128)}), f32[1,2,128,128]{3,2,1,0:T(8,128)S(1)}, s32[]{:S(2)}) async-start(f32[4,2,128,128]{3,2,1,0:T(8,128)} %copy-done.3), calls=%async_computation.4 | async-start | bytes 262144 | tf_op jit(solution)/shard_map/slice | solution.py:134
  127.2 104.0 %all-gather.4.cloned.1.call-start = ((), (), s32[]{:S(2)}) async-start(), calls=%async_computation | async-start | bytes 2228224 | tf_op jit(solution)/shard_map/all_gather | solution.py:21
  128.1 2.1 copy-start.17
  128.4 0.7 copy-start.16
  135.5 9.5 %copy-start.21 = (f32[1,2,128,128]{3,2,1,0:T(8,128)S(1)}, f32[1,2,128,128]{3,2,1,0:T(8,128)}, u32[]{:S(2)}) copy-start(f32[1,2,128,128]{3,2,1,0:T(8,128)} %slice.320) | copy-start | bytes 393220
  153.2 210.5 %all-reduce.15.cloned.1.call-start = ((), (), s32[]{:S(2)}) async-start(), calls=%async_computation.2 | async-start | bytes 524288 | tf_op jit(solution)/shard_map/psum | solution.py:34
  159.1 7.5 %slice-start.1 = ((f32[8,2,128,128]{3,2,1,0:T(8,128)}), f32[1,2,128,128]{3,2,1,0:T(8,128)S(1)}, s32[]{:S(2)}) async-start(f32[8,2,128,128]{3,2,1,0:T(8,128)} %copy-done.8), calls=%async_computation.5 | async-start | bytes 262144 | tf_op jit(solution)/shard_map/slice | solution.py:134
  164.8 8.4 %copy-start.27 = (f32[2,128]{1,0:T(2,128)S(1)}, f32[2,128]{1,0:T(2,128)}, u32[]{:S(2)}) copy-start(f32[2,128]{1,0:T(2,128)} %get-tuple-element.114) | copy-start | bytes 3076
  164.8 8.4 %copy-start.28 = (f32[2,128]{1,0:T(2,128)S(1)}, f32[2,128]{1,0:T(2,128)}, u32[]{:S(2)}) copy-start(f32[2,128]{1,0:T(2,128)} %get-tuple-element.121) | copy-start | bytes 3076
  164.8 8.4 %copy-start.29 = (f32[2,128]{1,0:T(2,128)S(1)}, f32[2,128]{1,0:T(2,128)}, u32[]{:S(2)}) copy-start(f32[2,128]{1,0:T(2,128)} %get-tuple-element.122) | copy-start | bytes 3076
  164.8 8.4 %copy-start.30 = (f32[2,128]{1,0:T(2,128)S(1)}, f32[2,128]{1,0:T(2,128)}, u32[]{:S(2)}) copy-start(f32[2,128]{1,0:T(2,128)} %get-tuple-element.123) | copy-start | bytes 3076
  166.6 8.9 %copy-start.7 = (bf16[512,2,128]{2,0,1:T(8,128)(2,1)S(1)}, bf16[512,2,128]{2,0,1:T(8,128)(2,1)}, u32[]{:S(2)}) copy-start(bf16[512,2,128]{2,0,1:T(8,128)(2,1)} %copy-done.6) | copy-start | bytes 786436
  166.6 8.9 %copy-start.24 = (pred[64,64]{1,0:T(8,128)(4,1)S(1)}, pred[64,64]{1,0:T(8,128)(4,1)}, u32[]{:S(2)}) copy-start(pred[64,64]{1,0:T(8,128)(4,1)} %copy-done.23) | copy-start | bytes 12292
  166.6 8.9 %copy-start.26 = (f32[8,2,64]{2,1,0:T(2,128)S(1)}, f32[8,2,64]{2,1,0:T(2,128)}, u32[]{:S(2)}) copy-start(f32[8,2,64]{2,1,0:T(2,128)} %copy-done.25) | copy-start | bytes 12292
  167.5 9.2 %copy-start.2 = (f32[8,2,64,256]{3,2,1,0:T(8,128)S(1)}, f32[8,2,64,256]{3,2,1,0:T(8,128)}, u32[]{:S(2)}) copy-start(f32[8,2,64,256]{3,2,1,0:T(8,128)} %copy-done.1) | copy-start | bytes 3145732
  167.5 9.2 %copy-start.32 = (f32[8]{0:T(128)S(1)}, f32[8]{0:T(128)}, u32[]{:S(2)}) copy-start(f32[8]{0:T(128)} %subtract_convert_fusion) | copy-start | bytes 100
  175.3 2.1 copy-start.9
  175.3 2.1 copy-start.13
  175.8 0.8 copy-start.15
  176.6 0.9 copy-start.20
  177.3 2.0 copy-start.4
  177.3 2.0 copy-start.10
  177.4 2.0 copy-start.11
  231.2 29.9 %copy-start.14 = (f32[1,2,128,128]{3,2,1,0:T(8,128)S(1)}, f32[1,2,128,128]{3,2,1,0:T(8,128)}, u32[]{:S(2)}) copy-start(f32[1,2,128,128]{3,2,1,0:T(8,128)} %slice_add_fusion.1) | copy-start | bytes 393220
  263.3 151.9 %all-gather.8.cloned.1.call-start = ((), (), s32[]{:S(2)}) async-start(), calls=%async_computation.3 | async-start | bytes 2359296 | tf_op jit(solution)/shard_map/all_gather | solution.py:164
  368.7 2.1 copy-start.5
  368.7 2.0 copy-start.12
  370.8 2.3 copy-start.22
  370.8 2.3 copy-start.33
Sparse Core Ops, SparseCore 0:
  127.3 51.9 all-gather.5
  181.8 49.3 all-gather.3
  263.4 100.2 all-reduce.14
  374.2 40.9 all-gather.7
where the time goes:
time: 433 us; the launch traced here: 429 us
  waiting for transfers between devices  190 us (44%)
  other arithmetic  97.6 us (23%)
  local copies, waits for them, and re-layouts  62.4 us (14%)
  matrix products  57.3 us (13%)
  between operations  13.9 us (3%)
    psum x1, waiting for transfers between devices, from_root(): return lax.psum(jnp.where(mine, shard, jnp.zeros_like(shard)), axis)  97.9 us
    another operation x3, other arithmetic, on_device(): jax.scipy.linalg.solve_triangular(jnp.eye(BLOCK, dtype=jnp.float32) + low...  79.4 us
    all_gather x2, waiting for transfers between devices, prefix(): gathered = jax.tree.map(lambda a: lax.all_gather(a, axis), part)  50.7 us
    all_gather x1, waiting for transfers between devices, on_device(): shard_piece = lax.all_gather(normed, 'head', axis=1, tiled=True)  41.1 us
    pad x8, local copies, waits for them, and re-layouts, on_device(): lax.associative_scan(chain_pair, (transition, addition), axis=0)  34.7 us
    dot_general x18, matrix products, chain_pair(): jnp.einsum('...ij,...jk->...ik', later_pair[0], earlier[1], precision=hig...  19.4 us
    dot_general x18, matrix products, chain_pair(): jnp.einsum('...ij,...jk->...ik', later_pair[0], earlier[0], precision=hig...  18.5 us
    unnamed x72, local copies, waits for them, and re-layouts  11.1 us
  transfers between devices with their start and end apart: 5, of which 3 were waited for; matrix products, arithmetic and copies ran while one was open for 14% of the time, Pallas kernels for 0%

commit v1 on v0

--- a/solution.py
+++ b/solution.py
@@ -8,6 +8,11 @@
 
 highest = lax.Precision.HIGHEST
 epsilon = 1e-06
+SEQ = ("chain", "leaf")
+
+
+def mm(spec, a, b):
+    return jnp.einsum(spec, a, b, precision=highest, preferred_element_type=jnp.float32)
 
 
 def from_behind(value, axis, steps):
@@ -16,35 +21,8 @@
     return lax.ppermute(value, axis, [(source, source + steps) for source in range(initial, last)])
 
 
-def prefix(part, axis, combine, identity):
-    place = lax.axis_index(axis)
-    gathered = jax.tree.map(lambda a: lax.all_gather(a, axis), part)
-    state = jax.tree.map(lambda a, e: jnp.zeros_like(a) + jnp.asarray(e, a.dtype), part, identity)
-
-    def one(lap, state):
-        return combine(
-            state, jax.tree.map(lambda a: lax.dynamic_index_in_dim(a, lap, 0, False), gathered)
-        )
-
-    return lax.fori_loop(0, place, one, state)
-
-
-def from_root(shard, axis, root):
-    mine = lax.axis_index(axis) == root
-    return lax.psum(jnp.where(mine, shard, jnp.zeros_like(shard)), axis)
-
-
 def unit_rows(matrix):
     return matrix / jnp.sqrt(jnp.sum(matrix * matrix, axis=-1, keepdims=True) + epsilon)
-
-
-def chain_pair(earlier, later_pair):
-    joined = jnp.einsum("...ij,...jk->...ik", later_pair[0], earlier[0], precision=highest)
-    carried = (
-        jnp.einsum("...ij,...jk->...ik", later_pair[0], earlier[1], precision=highest)
-        + later_pair[1]
-    )
-    return (joined, carried)
 
 
 def causal_filter(signal, rim_rows, weights):
@@ -55,6 +33,23 @@
     for offset in range(1, kernel):
         running = running + weights[offset] * padded[offset : offset + length]
     return jax.nn.silu(running)
+
+
+def unit_lower_inverse(lower):
+    size = lower.shape[-1]
+    row = lax.broadcasted_iota(jnp.int32, (size, size), 0)
+    col = lax.broadcasted_iota(jnp.int32, (size, size), 1)
+    inverse = jnp.broadcast_to(jnp.eye(size, dtype=jnp.float32), lower.shape)
+    span = 1
+    while span < size:
+        pick = ((row // (2 * span)) == (col // (2 * span))) & ((row // span) % 2 == 1) & (
+            (col // span) % 2 == 0
+        )
+        coupling = jnp.where(pick, lower, 0.0)
+        inverse = lax.optimization_barrier(inverse)
+        inverse = inverse - mm("...ij,...jk->...ik", mm("...ij,...jk->...ik", inverse, coupling), inverse)
+        span *= 2
+    return inverse
 
 
 def on_device(
@@ -79,7 +74,7 @@
             value_in[length - kernel + 1 :],
         ]
     )
-    rim_rows = from_behind(tail_rows, ("chain", "leaf"), 1)
+    rim_rows = from_behind(tail_rows, SEQ, 1)
     query_conv = causal_filter(query_in, rim_rows[0], conv_weight[0])
     key_conv = causal_filter(key_in, rim_rows[1], conv_weight[1])
     value_conv = causal_filter(value_in, rim_rows[2], conv_weight[2])
@@ -112,9 +107,7 @@
     targets = jnp.concatenate(
         [strength[..., None] * value_float, (strength * growth)[..., None] * key_float], axis=-1
     )
-    solved = jax.scipy.linalg.solve_triangular(
-        jnp.eye(BLOCK, dtype=jnp.float32) + lower, targets, lower=True, unit_diagonal=True
-    )
+    solved = mm("nhts,nhsf->nhtf", unit_lower_inverse(lower), targets)
     local_values = solved[..., :value_width]
     write_keys = solved[..., value_width:]
     tail_fade = jnp.exp(cumulative[..., -1:] - cumulative)
@@ -123,39 +116,44 @@
     keep_mat = (1 - doc_resets).astype(jnp.float32)[:, None, None, None]
     transition = keep_mat * (
         growth[..., -1, None, None] * key_eye
-        - jnp.einsum("nhce,nhcf->nhef", decayed_addresses, write_keys, precision=highest)
+        - mm("nhce,nhcf->nhef", decayed_addresses, write_keys)
     )
-    addition = jnp.einsum("nhce,nhcf->nhef", decayed_addresses, local_values, precision=highest)
+    addition = mm("nhce,nhcf->nhef", decayed_addresses, local_values)
     query_eff = keep_mat * (
-        growth[..., None] * query_float
-        - jnp.einsum("nhts,nhse->nhte", mixing, write_keys, precision=highest)
+        growth[..., None] * query_float - mm("nhts,nhse->nhte", mixing, write_keys)
     )
-    own_output = jnp.einsum("nhts,nhsf->nhtf", mixing, local_values, precision=highest)
-    prefix_trans, prefix_state = lax.associative_scan(chain_pair, (transition, addition), axis=0)
-    start_trans = jnp.concatenate(
-        [jnp.broadcast_to(key_eye, (1, head_count, depth_k, depth_k)), prefix_trans[:-1]], axis=0
+    own_output = mm("nhts,nhsf->nhtf", mixing, local_values)
+    carry = jnp.concatenate(
+        [
+            jnp.broadcast_to(key_eye, (head_count, depth_k, depth_k)),
+            jnp.zeros((head_count, depth_k, value_width), jnp.float32),
+        ],
+        axis=-1,
     )
-    start_state = jnp.concatenate(
-        [jnp.zeros((1, head_count, depth_k, value_width), jnp.float32), prefix_state[:-1]], axis=0
-    )
-    device_trans = prefix_trans[-1]
-    device_state = prefix_state[-1]
-    partial_out = own_output + jnp.einsum(
-        "nhtd,nhdf->nhtf", query_eff, start_state, precision=highest
-    )
-    reach_map = jnp.einsum("nhtd,nhde->nhte", query_eff, start_trans, precision=highest)
-    identity_pair = (
-        jnp.broadcast_to(key_eye, (head_count, depth_k, depth_k)),
-        jnp.zeros((head_count, depth_k, value_width), jnp.float32),
-    )
-    leaf_trans, leaf_state = prefix((device_trans, device_state), "leaf", chain_pair, identity_pair)
-    through = chain_pair((leaf_trans, leaf_state), (device_trans, device_state))
-    group_pair = from_root(jnp.stack(through), "leaf", lax.axis_size("leaf") - 1)
-    outer_trans, outer_state = prefix(
-        (group_pair[0], group_pair[1]), "chain", chain_pair, identity_pair
-    )
-    incoming = jnp.einsum("hij,hjk->hik", leaf_trans, outer_state, precision=highest) + leaf_state
-    core = partial_out + jnp.einsum("nhte,hef->nhtf", reach_map, incoming, precision=highest)
+    starts = []
+    for n in range(blocks):
+        starts.append(carry)
+        carry = mm("hij,hjk->hik", transition[n], carry)
+        carry = carry.at[..., depth_k:].add(addition[n])
+    starts = jnp.stack(starts)
+    reach = mm("nhtd,nhde->nhte", query_eff, starts)
+    partial_out = own_output + reach[..., depth_k:]
+    reach_map = reach[..., :depth_k]
+    device_trans = carry[..., :depth_k]
+    device_state = carry[..., depth_k:]
+    place = lax.axis_index(SEQ)
+    count = lax.axis_size(SEQ)
+    trans, state = device_trans, device_state
+    stride = 1
+    while stride < count:
+        got_trans, got_state = from_behind((trans, state), SEQ, stride)
+        has = place >= stride
+        state = state + mm("hij,hjk->hik", trans, got_state)
+        if stride * 2 < count:
+            trans = jnp.where(has, mm("hij,hjk->hik", trans, got_trans), trans)
+        stride *= 2
+    incoming = from_behind(state, SEQ, 1)
+    core = partial_out + mm("nhte,hef->nhtf", reach_map, incoming)
     core = jnp.transpose(core, (0, 2, 1, 3)).reshape(length, head_count, value_width)
     scale_rms = jnp.sqrt(jnp.mean(core * core, axis=-1, keepdims=True) + epsilon)
     normed = (

time: 433 us -> 158 us (0.36)
  waiting for transfers between devices: 190 us -> 63.2 us
  other arithmetic: 97.6 us -> 8.9 us
  local copies, waits for them, and re-layouts: 62.4 us -> 16.7 us
  matrix products: 57.3 us -> 25.9 us
  starting transfers between devices: 3.71 us -> 27.7 us
    psum x1 -> x0, waiting for transfers between devices: 97.9 us -> none  [from_root(): return lax.psum(jnp.where(mine, shard, jnp.zeros_like(shard)), axis)]
    another operation x3 -> x0, other arithmetic: 79.4 us -> none  [on_device(): jax.scipy.linalg.solve_triangular(jnp.eye(BLOCK, dtype=jnp.float32) + low...]
    all_gather x2 -> x0, waiting for transfers between devices: 50.7 us -> none  [prefix(): gathered = jax.tree.map(lambda a: lax.all_gather(a, axis), part)]
    pad x8 -> x0, local copies, waits for them, and re-layouts: 34.7 us -> none  [on_device(): lax.associative_scan(chain_pair, (transition, addition), axis=0)]
    dot_general x44 -> x36, matrix products: 51.1 us -> 21.7 us  [mm(): jnp.einsum(spec, a, b, precision=highest, preferred_element_type=jnp.floa...]
    ppermute x1 -> x11, starting transfers between devices: 3.4 us -> 27.7 us  [from_behind(): lax.ppermute(value, axis, [(source, source + steps) for source in range(i...]
    ppermute x1 -> x11, waiting for transfers between devices: 0.01 us -> 21.7 us  [from_behind(): lax.ppermute(value, axis, [(source, source + steps) for source in range(i...]
    slice x11 -> x0, local copies, waits for them, and re-layouts: 8.93 us -> none  [the longest x1 5.69 us: on_device(): prefix_trans[:-1]]
  transfers between devices with their start and end apart: 5 -> 12, of which waited for: 3 -> 8; matrix products, arithmetic and copies ran while one was open for 14% -> 12% of each run, Pallas kernels for 0% -> 0%
where the time goes in v1:
time: 158 us; the launch traced here: 157 us
  waiting for transfers between devices  63.2 us (40%)
  starting transfers between devices  27.7 us (18%)
  matrix products  25.9 us (16%)
  local copies, waits for them, and re-layouts  16.7 us (11%)
  between operations  14.4 us (9%)
  other arithmetic  8.9 us (6%)
    all_gather x1, waiting for transfers between devices, on_device(): shard_piece = lax.all_gather(normed, 'head', axis=1, tiled=True)  41.5 us
    ppermute x11, starting transfers between devices, from_behind(): lax.ppermute(value, axis, [(source, source + steps) for source in range(i...  27.7 us
    ppermute x11, waiting for transfers between devices, from_behind(): lax.ppermute(value, axis, [(source, source + steps) for source in range(i...  21.7 us
    dot_general x36, matrix products, mm(): jnp.einsum(spec, a, b, precision=highest, preferred_element_type=jnp.floa...  21.7 us
    unnamed x56, local copies, waits for them, and re-layouts  4.06 us
    all_gather x1, local copies, waits for them, and re-layouts, on_device(): shard_piece = lax.all_gather(normed, 'head', axis=1, tiled=True)  3.93 us
    dot_general x1, matrix products, on_device(): jnp.dot(flat_piece, output_projection_weight, preferred_element_type=jnp....  3.66 us
  transfers between devices with their start and end apart: 12, of which 8 were waited for; matrix products, arithmetic and copies ran while one was open for 12% of the time, Pallas kernels for 0%

profile of v1, /device:TPU:24, one launch (start us, length us, event | category | flops | bytes accessed | tf_op | source)
XLA Modules:
  0.0 156.8 jit_solution(13814795067078425158)
XLA Ops:
  6.5 1.1 copy.162
  7.7 1.0 copy.161
  8.7 1.0 copy.160
  9.7 0.6 pad_maximum_fusion.3
  10.3 3.4 %collective-permute-start = (bf16[3,3,2,128]{3,1,2,0:T(4,128)(2,1)}, bf16[3,3,2,128]{3,1,2,0:T(4,128)(2,1)}, u32[]{:S(2)}, u32[]{:S(2)}) collective-permute-start(bf16[3,3,2,128]{3,1,2,0:T(4,128)(2,1)} %pad_maximum_fusion.3), channel_id=1, source_target_pairs={{0,8},{8,16},{16,24},{24,32},{32,40},{40,48},{48,56},{56,64},{64,7... | collective-permute-start | bytes 13832 | tf_op jit(solution)/shard_map/ppermute | solution.py:21
  13.8 0.6 fusion.123
  14.5 1.5 slice_bitcast_fusion.33
  15.9 0.8 reshape.339
  16.7 0.8 reshape.342
  17.5 0.4 reduce_window_sum.11
  18.1 1.1 subtract_convert_fusion
  19.2 0.7 fusion.41
  20.0 0.7 subtract_exponential_fusion
  20.6 0.8 fusion.122
  21.4 0.6 iota_compare_fusion.1
  22.1 0.6 copy.158
  22.7 0.6 copy.178
  23.3 0.6 copy.169
  23.9 0.8 broadcast_in_dim.62
  24.7 0.6 copy.176
  25.3 0.7 copy.186
  26.1 0.7 copy.181
  26.8 0.7 slice_bitcast_fusion.24
  27.5 1.4 multiply_reduce_fusion.1
  29.6 0.7 fusion.26
  30.3 0.6 convolution_subtract_fusion.6
  31.0 0.7 fusion.24
  31.6 0.6 convolution_subtract_fusion.5
  32.3 0.7 fusion.22
  33.0 0.6 convolution_subtract_fusion.4
  33.6 0.7 fusion.20
  34.3 0.6 convolution_subtract_fusion.3
  34.9 0.7 fusion.18
  35.6 0.6 convolution_subtract_fusion.2
  36.3 0.7 fusion.16
  36.9 0.6 convolution_subtract_fusion.1
  38.0 1.0 fusion.5
  39.0 2.2 %fusion.15 = f32[8,2,128,128]{3,2,1,0:T(8,128)S(1)} fusion(f32[8,2,64,256]{3,2,1,0:T(8,128)S(1)} %fusion.5, f32[8,2,64]{2,1,0:T(2,128)S(1)} %copy.181, bf16[8,64,2,128]{3,1,0,2:T(8,128)(2,1)S(1)} %bitcast.218), kind=kOutput, calls=%fused_computation.43 | convolution fusion | flops 201588736 | bytes 1843200 | tf_op jit(solution)/shard_map/nhce,nhcf->nhef/dot_general | solution.py:15
  41.3 2.0 %fusion = f32[8,2,128,128]{3,2,1,0:T(8,128)S(1)} fusion(f32[128,128]{1,0:T(8,128)S(1)} %copy-done.3, f32[8,2]{1,0:T(8,128)S(1)} %bitcast.226, f32[8]{0:T(128)S(1)} %copy-done.21, f32[8,2,64,256]{3,2,1,0:T(8,128)S(1)} %fusion.5, f32[8,2,64]{2,1,0:T(2,128)S(1)} %copy.181, bf16[8,64,2,128]{3,1,0,2:T(8,128)(2,1)S(1)} %bitcast.219), kind=kOutput, calls=%fused_computation.1 | convolution fusion | flops 202375168 | bytes 1913344 | tf_op jit(solution)/shard_map/nhce,nhcf->nhef/dot_general | solution.py:15
  46.6 3.4 %collective-permute-start.2 = (f32[2,128,128]{2,1,0:T(8,128)S(1)}, f32[2,128,128]{2,1,0:T(8,128)S(1)}, u32[]{:S(2)}, u32[]{:S(2)}) collective-permute-start(f32[2,128,128]{2,1,0:T(8,128)S(1)} %get-tuple-element.105), channel_id=1, source_target_pairs={{0,8},{8,16},{16,24},{24,32},{32,40},{40,48},{48,56},{56,64},{64,7... | collective-permute-start | bytes 393224 | tf_op jit(solution)/shard_map/ppermute | solution.py:21
  50.0 3.1 %collective-permute-start.1 = (f32[2,128,128]{2,1,0:T(8,128)S(1)}, f32[2,128,128]{2,1,0:T(8,128)S(1)}, u32[]{:S(2)}, u32[]{:S(2)}) collective-permute-start(f32[2,128,128]{2,1,0:T(8,128)S(1)} %get-tuple-element.106), channel_id=1, source_target_pairs={{0,8},{8,16},{16,24},{24,32},{32,40},{40,48},{48,56},{56,64},{64,7... | collective-permute-start | bytes 393224 | tf_op jit(solution)/shard_map/ppermute | solution.py:21
  53.3 0.5 multiply_reduce_fusion.2
  54.3 0.7 fusion.1
  55.0 1.3 fusion.140
  56.3 2.6 %collective-permute-done.1 = f32[2,128,128]{2,1,0:T(8,128)S(1)} collective-permute-done((f32[2,128,128]{2,1,0:T(8,128)S(1)}, f32[2,128,128]{2,1,0:T(8,128)S(1)}, u32[]{:S(2)}, u32[]{:S(2)}) %collective-permute-start.1) | collective-permute-done | bytes 131104 | tf_op jit(solution)/shard_map/ppermute | solution.py:21
  59.2 1.9 %collective-permute-start.3 = (f32[2,128,128]{2,1,0:T(8,128)S(1)}, f32[2,128,128]{2,1,0:T(8,128)S(1)}, u32[]{:S(2)}, u32[]{:S(2)}) collective-permute-start(f32[2,128,128]{2,1,0:T(8,128)S(1)} %convolution_add_fusion.5), channel_id=1, source_target_pairs={{0,16},{8,24},{16,32},{24,40},{32,48},{40,56},{48,64},{56,72},{64,... | collective-permute-start | bytes 393224 | tf_op jit(solution)/shard_map/ppermute | solution.py:21
  61.4 4.6 %collective-permute-start.4 = (f32[2,128,128]{2,1,0:T(8,128)S(1)}, f32[2,128,128]{2,1,0:T(8,128)S(1)}, u32[]{:S(2)}, u32[]{:S(2)}) collective-permute-start(f32[2,128,128]{2,1,0:T(8,128)S(1)} %convolution_select_fusion.3), channel_id=1, source_target_pairs={{0,16},{8,24},{16,32},{24,40},{32,48},{40,56},{48,64},{56,72},{64,... | collective-permute-start | bytes 393224 | tf_op jit(solution)/shard_map/ppermute | solution.py:21
  66.0 3.7 %collective-permute-done.3 = f32[2,128,128]{2,1,0:T(8,128)S(1)} collective-permute-done((f32[2,128,128]{2,1,0:T(8,128)S(1)}, f32[2,128,128]{2,1,0:T(8,128)S(1)}, u32[]{:S(2)}, u32[]{:S(2)}) %collective-permute-start.3) | collective-permute-done | bytes 131104 | tf_op jit(solution)/shard_map/ppermute | solution.py:21
  70.0 1.9 %collective-permute-start.5 = (f32[2,128,128]{2,1,0:T(8,128)S(1)}, f32[2,128,128]{2,1,0:T(8,128)S(1)}, u32[]{:S(2)}, u32[]{:S(2)}) collective-permute-start(f32[2,128,128]{2,1,0:T(8,128)S(1)} %convolution_add_fusion.4), channel_id=1, source_target_pairs={{0,32},{8,40},{16,48},{24,56},{32,64},{40,72},{48,80},{56,88},{64,... | collective-permute-start | bytes 393224 | tf_op jit(solution)/shard_map/ppermute | solution.py:21
  72.2 1.9 %collective-permute-start.6 = (f32[2,128,128]{2,1,0:T(8,128)S(1)}, f32[2,128,128]{2,1,0:T(8,128)S(1)}, u32[]{:S(2)}, u32[]{:S(2)}) collective-permute-start(f32[2,128,128]{2,1,0:T(8,128)S(1)} %convolution_select_fusion.2), channel_id=1, source_target_pairs={{0,32},{8,40},{16,48},{24,56},{32,64},{40,72},{48,80},{56,88},{64,... | collective-permute-start | bytes 393224 | tf_op jit(solution)/shard_map/ppermute | solution.py:21
  74.1 3.5 %collective-permute-done.5 = f32[2,128,128]{2,1,0:T(8,128)S(1)} collective-permute-done((f32[2,128,128]{2,1,0:T(8,128)S(1)}, f32[2,128,128]{2,1,0:T(8,128)S(1)}, u32[]{:S(2)}, u32[]{:S(2)}) %collective-permute-start.5) | collective-permute-done | bytes 131104 | tf_op jit(solution)/shard_map/ppermute | solution.py:21
  78.0 1.9 %collective-permute-start.7 = (f32[2,128,128]{2,1,0:T(8,128)S(1)}, f32[2,128,128]{2,1,0:T(8,128)S(1)}, u32[]{:S(2)}, u32[]{:S(2)}) collective-permute-start(f32[2,128,128]{2,1,0:T(8,128)S(1)} %convolution_add_fusion.3), channel_id=1, source_target_pairs={{0,64},{8,72},{16,80},{24,88},{32,96},{40,104},{48,112},{56,120},{... | collective-permute-start | bytes 393224 | tf_op jit(solution)/shard_map/ppermute | solution.py:21
  80.2 1.9 %collective-permute-start.8 = (f32[2,128,128]{2,1,0:T(8,128)S(1)}, f32[2,128,128]{2,1,0:T(8,128)S(1)}, u32[]{:S(2)}, u32[]{:S(2)}) collective-permute-start(f32[2,128,128]{2,1,0:T(8,128)S(1)} %convolution_select_fusion.1), channel_id=1, source_target_pairs={{0,64},{8,72},{16,80},{24,88},{32,96},{40,104},{48,112},{56,120},{... | collective-permute-start | bytes 393224 | tf_op jit(solution)/shard_map/ppermute | solution.py:21
  82.1 4.2 %collective-permute-done.7 = f32[2,128,128]{2,1,0:T(8,128)S(1)} collective-permute-done((f32[2,128,128]{2,1,0:T(8,128)S(1)}, f32[2,128,128]{2,1,0:T(8,128)S(1)}, u32[]{:S(2)}, u32[]{:S(2)}) %collective-permute-start.7) | collective-permute-done | bytes 131104 | tf_op jit(solution)/shard_map/ppermute | solution.py:21
  86.6 1.3 collective-permute-start.9
  87.9 0.6 collective-permute-done.8
  89.2 2.3 %collective-permute-start.10 = (f32[2,128,128]{2,1,0:T(8,128)S(1)}, f32[2,128,128]{2,1,0:T(8,128)S(1)}, u32[]{:S(2)}, u32[]{:S(2)}) collective-permute-start(f32[2,128,128]{2,1,0:T(8,128)S(1)} %convolution_add_fusion.1), channel_id=1, source_target_pairs={{0,8},{8,16},{16,24},{24,32},{32,40},{40,48},{48,56},{56,64},{64,7... | collective-permute-start | bytes 393224 | tf_op jit(solution)/shard_map/ppermute | solution.py:21
  91.4 0.7 convolution_add_fusion
  92.1 7.0 %collective-permute-done.10 = f32[2,128,128]{2,1,0:T(8,128)S(1)} collective-permute-done((f32[2,128,128]{2,1,0:T(8,128)S(1)}, f32[2,128,128]{2,1,0:T(8,128)S(1)}, u32[]{:S(2)}, u32[]{:S(2)}) %collective-permute-start.10) | collective-permute-done | bytes 131104 | tf_op jit(solution)/shard_map/ppermute | solution.py:21
  99.1 0.8 multiply_reduce_fusion
  100.0 0.9 fusion.28
  100.9 41.5 %all-gather.2.cloned.1.call-done = bf16[512,16,128]{2,0,1:T(8,128)(2,1)} async-done(((bf16[512,2,128]{2,0,1:T(8,128)(2,1)}), bf16[512,16,128]{2,0,1:T(8,128)(2,1)}) %all-gather.2.cloned.1.call-update) | async-done | bytes 2097168 | tf_op jit(solution)/shard_map/all_gather | solution.py:162
  142.4 3.9 %copy.185 = bf16[512,16,128]{0,2,1:T(8,128)(2,1)} copy(bf16[512,16,128]{2,0,1:T(8,128)(2,1)} %all-gather.2.cloned.1.call-done) | data formatting | bytes 4194304 | tf_op jit(solution)/shard_map/all_gather | solution.py:162
  146.3 3.7 %convolution_convert_fusion = bf16[512,512]{1,0:T(8,128)(2,1)} fusion(bf16[512,2048]{0,1:T(8,128)(2,1)} %bitcast.215, bf16[2048,512]{1,0:T(8,128)(2,1)S(1)} %copy-done), kind=kOutput, calls=%fused_computation.2 | convolution fusion | flops 1074003968 | bytes 4718592 | tf_op jit(solution)/shard_map/dot_general | solution.py:165
  (112 shorter events, 7.7 us)
Async XLA Ops:
  6.5 139.8 %copy-start = (bf16[2048,512]{1,0:T(8,128)(2,1)S(1)}, bf16[2048,512]{1,0:T(8,128)(2,1)}, u32[]{:S(2)}) copy-start(bf16[2048,512]{1,0:T(8,128)(2,1)} %param.35) | copy-start | bytes 6291460
  6.5 135.9 %all-gather.2.cloned.1.call-start = ((), (), s32[]{:S(2)}) async-start(), calls=%async_computation | async-start | bytes 2359296 | tf_op jit(solution)/shard_map/all_gather | solution.py:162
  10.3 16.5 %collective-permute-start = (bf16[3,3,2,128]{3,1,2,0:T(4,128)(2,1)}, bf16[3,3,2,128]{3,1,2,0:T(4,128)(2,1)}, u32[]{:S(2)}, u32[]{:S(2)}) collective-permute-start(bf16[3,3,2,128]{3,1,2,0:T(4,128)(2,1)} %pad_maximum_fusion.3), channel_id=1, source_target_pairs={{0,8},{8,16},{16,24},{24,32},{32,40},{40,48},{48,56},{56,64},{64,7... | collective-permute-start | bytes 13832 | tf_op jit(solution)/shard_map/ppermute | solution.py:21
  14.4 8.9 %copy-start.2 = (f32[128,128]{1,0:T(8,128)}, f32[128,128]{1,0:T(8,128)S(1)}, u32[]{:S(2)}) copy-start(f32[128,128]{1,0:T(8,128)S(1)} %fusion.84) | copy-start | bytes 196612
  26.8 2.4 %copy-start.11 = (f32[8,2,64]{2,1,0:T(2,128)S(1)}, f32[8,2,64]{2,1,0:T(2,128)}, u32[]{:S(2)}) copy-start(f32[8,2,64]{2,1,0:T(2,128)} %copy.169) | copy-start | bytes 12292
  26.8 2.4 %copy-start.14 = (pred[64,64]{1,0:T(8,128)(4,1)S(1)}, pred[64,64]{1,0:T(8,128)(4,1)}, u32[]{:S(2)}) copy-start(pred[64,64]{1,0:T(8,128)(4,1)} %get-tuple-element.135) | copy-start | bytes 12292
  26.8 2.4 %copy-start.15 = (f32[8,2,64]{2,1,0:T(2,128)S(1)}, f32[8,2,64]{2,1,0:T(2,128)}, u32[]{:S(2)}) copy-start(f32[8,2,64]{2,1,0:T(2,128)} %copy.158) | copy-start | bytes 12292
  26.8 2.4 %copy-start.16 = (pred[64,64]{1,0:T(8,128)(4,1)S(1)}, pred[64,64]{1,0:T(8,128)(4,1)}, u32[]{:S(2)}) copy-start(pred[64,64]{1,0:T(8,128)(4,1)} %get-tuple-element.134) | copy-start | bytes 12292
  26.8 2.8 %copy-start.9 = (pred[64,64]{1,0:T(8,128)(4,1)S(1)}, pred[64,64]{1,0:T(8,128)(4,1)}, u32[]{:S(2)}) copy-start(pred[64,64]{1,0:T(8,128)(4,1)} %get-tuple-element.130) | copy-start | bytes 12292
  29.2 1.7 %copy-start.8 = (pred[64,64]{1,0:T(8,128)(4,1)S(1)}, pred[64,64]{1,0:T(8,128)(4,1)}, u32[]{:S(2)}) copy-start(pred[64,64]{1,0:T(8,128)(4,1)} %get-tuple-element.129) | copy-start | bytes 12292
  30.3 2.0 %copy-start.7 = (pred[64,64]{1,0:T(8,128)(4,1)S(1)}, pred[64,64]{1,0:T(8,128)(4,1)}, u32[]{:S(2)}) copy-start(pred[64,64]{1,0:T(8,128)(4,1)} %get-tuple-element.128) | copy-start | bytes 12292
  31.6 2.0 %copy-start.6 = (pred[64,64]{1,0:T(8,128)(4,1)S(1)}, pred[64,64]{1,0:T(8,128)(4,1)}, u32[]{:S(2)}) copy-start(pred[64,64]{1,0:T(8,128)(4,1)} %get-tuple-element.127) | copy-start | bytes 12292
  32.9 2.0 %copy-start.5 = (pred[64,64]{1,0:T(8,128)(4,1)S(1)}, pred[64,64]{1,0:T(8,128)(4,1)}, u32[]{:S(2)}) copy-start(pred[64,64]{1,0:T(8,128)(4,1)} %get-tuple-element.126) | copy-start | bytes 12292
  35.6 2.0 %copy-start.12 = (f32[8,2,64]{2,1,0:T(2,128)S(1)}, f32[8,2,64]{2,1,0:T(2,128)}, u32[]{:S(2)}) copy-start(f32[8,2,64]{2,1,0:T(2,128)} %copy.176) | copy-start | bytes 12292
  38.0 3.2 %copy-start.3 = (f32[128,128]{1,0:T(8,128)S(1)}, f32[128,128]{1,0:T(8,128)}, u32[]{:S(2)}) copy-start(f32[128,128]{1,0:T(8,128)} %copy-done.2) | copy-start | bytes 196612
  38.0 3.2 %copy-start.13 = (f32[8,2,1]{1,0,2:T(8,128)S(1)}, f32[8,2,1]{1,0,2:T(8,128)}, u32[]{:S(2)}) copy-start(f32[8,2,1]{1,0,2:T(8,128)} %copy.186) | copy-start | bytes 196
  38.0 3.2 %copy-start.21 = (f32[8]{0:T(128)S(1)}, f32[8]{0:T(128)}, u32[]{:S(2)}) copy-start(f32[8]{0:T(128)} %subtract_convert_fusion) | copy-start | bytes 100
  44.9 8.2 %copy-start.1 = (f32[8,2,128,256]{3,2,1,0:T(8,128)S(1)}, f32[8,2,128,256]{3,2,1,0:T(8,128)}, u32[]{:S(2)}) copy-start(f32[8,2,128,256]{3,2,1,0:T(8,128)} %fusion.41) | copy-start | bytes 6291460
  46.5 6.8 %copy-start.17 = (f32[2,128]{1,0:T(2,128)S(1)}, f32[2,128]{1,0:T(2,128)}, u32[]{:S(2)}) copy-start(f32[2,128]{1,0:T(2,128)} %get-tuple-element.113) | copy-start | bytes 3076
  46.5 6.8 %copy-start.18 = (f32[2,128]{1,0:T(2,128)S(1)}, f32[2,128]{1,0:T(2,128)}, u32[]{:S(2)}) copy-start(f32[2,128]{1,0:T(2,128)} %get-tuple-element.114) | copy-start | bytes 3076
  46.5 6.8 %copy-start.19 = (f32[2,128]{1,0:T(2,128)S(1)}, f32[2,128]{1,0:T(2,128)}, u32[]{:S(2)}) copy-start(f32[2,128]{1,0:T(2,128)} %get-tuple-element.115) | copy-start | bytes 3076
  46.5 6.8 %copy-start.20 = (f32[2,128]{1,0:T(2,128)S(1)}, f32[2,128]{1,0:T(2,128)}, u32[]{:S(2)}) copy-start(f32[2,128]{1,0:T(2,128)} %get-tuple-element.116) | copy-start | bytes 3076
  46.6 14.6 %collective-permute-start.2 = (f32[2,128,128]{2,1,0:T(8,128)S(1)}, f32[2,128,128]{2,1,0:T(8,128)S(1)}, u32[]{:S(2)}, u32[]{:S(2)}) collective-permute-start(f32[2,128,128]{2,1,0:T(8,128)S(1)} %get-tuple-element.105), channel_id=1, source_target_pairs={{0,8},{8,16},{16,24},{24,32},{32,40},{40,48},{48,56},{56,64},{64,7... | collective-permute-start | bytes 393224 | tf_op jit(solution)/shard_map/ppermute | solution.py:21
  50.0 9.0 %collective-permute-start.1 = (f32[2,128,128]{2,1,0:T(8,128)S(1)}, f32[2,128,128]{2,1,0:T(8,128)S(1)}, u32[]{:S(2)}, u32[]{:S(2)}) collective-permute-start(f32[2,128,128]{2,1,0:T(8,128)S(1)} %get-tuple-element.106), channel_id=1, source_target_pairs={{0,8},{8,16},{16,24},{24,32},{32,40},{40,48},{48,56},{56,64},{64,7... | collective-permute-start | bytes 393224 | tf_op jit(solution)/shard_map/ppermute | solution.py:21
  53.2 1.1 copy-start.10
  59.2 10.5 %collective-permute-start.3 = (f32[2,128,128]{2,1,0:T(8,128)S(1)}, f32[2,128,128]{2,1,0:T(8,128)S(1)}, u32[]{:S(2)}, u32[]{:S(2)}) collective-permute-start(f32[2,128,128]{2,1,0:T(8,128)S(1)} %convolution_add_fusion.5), channel_id=1, source_target_pairs={{0,16},{8,24},{16,32},{24,40},{32,48},{40,56},{48,64},{56,72},{64,... | collective-permute-start | bytes 393224 | tf_op jit(solution)/shard_map/ppermute | solution.py:21
  61.4 10.5 %collective-permute-start.4 = (f32[2,128,128]{2,1,0:T(8,128)S(1)}, f32[2,128,128]{2,1,0:T(8,128)S(1)}, u32[]{:S(2)}, u32[]{:S(2)}) collective-permute-start(f32[2,128,128]{2,1,0:T(8,128)S(1)} %convolution_select_fusion.3), channel_id=1, source_target_pairs={{0,16},{8,24},{16,32},{24,40},{32,48},{40,56},{48,64},{56,72},{64,... | collective-permute-start | bytes 393224 | tf_op jit(solution)/shard_map/ppermute | solution.py:21
  70.0 7.7 %collective-permute-start.5 = (f32[2,128,128]{2,1,0:T(8,128)S(1)}, f32[2,128,128]{2,1,0:T(8,128)S(1)}, u32[]{:S(2)}, u32[]{:S(2)}) collective-permute-start(f32[2,128,128]{2,1,0:T(8,128)S(1)} %convolution_add_fusion.4), channel_id=1, source_target_pairs={{0,32},{8,40},{16,48},{24,56},{32,64},{40,72},{48,80},{56,88},{64,... | collective-permute-start | bytes 393224 | tf_op jit(solution)/shard_map/ppermute | solution.py:21
  72.2 7.7 %collective-permute-start.6 = (f32[2,128,128]{2,1,0:T(8,128)S(1)}, f32[2,128,128]{2,1,0:T(8,128)S(1)}, u32[]{:S(2)}, u32[]{:S(2)}) collective-permute-start(f32[2,128,128]{2,1,0:T(8,128)S(1)} %convolution_select_fusion.2), channel_id=1, source_target_pairs={{0,32},{8,40},{16,48},{24,56},{32,64},{40,72},{48,80},{56,88},{64,... | collective-permute-start | bytes 393224 | tf_op jit(solution)/shard_map/ppermute | solution.py:21
  78.0 8.4 %collective-permute-start.7 = (f32[2,128,128]{2,1,0:T(8,128)S(1)}, f32[2,128,128]{2,1,0:T(8,128)S(1)}, u32[]{:S(2)}, u32[]{:S(2)}) collective-permute-start(f32[2,128,128]{2,1,0:T(8,128)S(1)} %convolution_add_fusion.3), channel_id=1, source_target_pairs={{0,64},{8,72},{16,80},{24,88},{32,96},{40,104},{48,112},{56,120},{... | collective-permute-start | bytes 393224 | tf_op jit(solution)/shard_map/ppermute | solution.py:21
  80.2 8.4 %collective-permute-start.8 = (f32[2,128,128]{2,1,0:T(8,128)S(1)}, f32[2,128,128]{2,1,0:T(8,128)S(1)}, u32[]{:S(2)}, u32[]{:S(2)}) collective-permute-start(f32[2,128,128]{2,1,0:T(8,128)S(1)} %convolution_select_fusion.1), channel_id=1, source_target_pairs={{0,64},{8,72},{16,80},{24,88},{32,96},{40,104},{48,112},{56,120},{... | collective-permute-start | bytes 393224 | tf_op jit(solution)/shard_map/ppermute | solution.py:21
  86.6 2.3 %collective-permute-start.9 = (f32[2,128,128]{2,1,0:T(8,128)S(1)}, f32[2,128,128]{2,1,0:T(8,128)S(1)}, u32[]{:S(2)}, u32[]{:S(2)}) collective-permute-start(f32[2,128,128]{2,1,0:T(8,128)S(1)} %convolution_add_fusion.2), channel_id=1, source_target_pairs={{0,128},{8,136},{16,144},{24,152},{32,160},{40,168},{48,176},{56,1... | collective-permute-start | bytes 393224 | tf_op jit(solution)/shard_map/ppermute | solution.py:21
  89.1 10.8 %copy-start.4 = (bf16[512,2,128]{2,1,0:T(2,128)(2,1)S(1)}, bf16[512,2,128]{2,1,0:T(2,128)(2,1)}, u32[]{:S(2)}) copy-start(bf16[512,2,128]{2,1,0:T(2,128)(2,1)} %param.29) | copy-start | bytes 786436
  89.1 10.8 %copy-start.22 = (f32[128]{0:T(128)S(1)}, f32[128]{0:T(128)}, u32[]{:S(2)}) copy-start(f32[128]{0:T(128)} %param.34) | copy-start | bytes 1540
  89.2 9.9 %collective-permute-start.10 = (f32[2,128,128]{2,1,0:T(8,128)S(1)}, f32[2,128,128]{2,1,0:T(8,128)S(1)}, u32[]{:S(2)}, u32[]{:S(2)}) collective-permute-start(f32[2,128,128]{2,1,0:T(8,128)S(1)} %convolution_add_fusion.1), channel_id=1, source_target_pairs={{0,8},{8,16},{16,24},{24,32},{32,40},{40,48},{48,56},{56,64},{64,7... | collective-permute-start | bytes 393224 | tf_op jit(solution)/shard_map/ppermute | solution.py:21
Sparse Core Ops, SparseCore 0:
  101.1 41.2 all-gather.1
